TPU v7x, 512 devices: a whole 4x4x16 slice. The times are simulated.
512 devices in a mesh: dp: 32 (over y_hi, z), expert: 16 (over y_lo, x, core).
Axes of the slice: x: 4, y: 4 (y_hi: 2, y_lo: 2; y = y_hi * 2 + y_lo), z: 16, core: 2. Of those that a mesh axis runs over, the one named last changes fastest.
Arguments:
- residual_in: bfloat16 [1536, 2048], P('dp', 'expert'), may hold values from -36 to 36
- attention_values: bfloat16 [1536, 2048], P('dp', 'expert'), may hold values from -6 to 6
- out_weight: bfloat16 [2048, 2048], P('expert', 'dp'), may hold values from -0.25 to 0.25
- norm_gain: float32 [2048], replicated, may hold values from 0.1 to 1.9
- shared_gate: bfloat16 [2816, 2048], P('expert'), may hold values from -0.125 to 0.125
- shared_up: bfloat16 [2816, 2048], P('expert'), may hold values from -0.125 to 0.125
- shared_down: bfloat16 [2816, 2048], P('expert'), may hold values from -0.15625 to 0.15625
- expert_gate: bfloat16 [64, 1408, 2048], P('dp', 'expert'), may hold values from -0.125 to 0.125
- expert_up: bfloat16 [64, 1408, 2048], P('dp', 'expert'), may hold values from -0.125 to 0.125
- expert_down: bfloat16 [64, 1408, 2048], P('dp', 'expert'), may hold values from -0.21875 to 0.21875
- expert_ids: int32 [1536, 6], P('dp'), may hold values from 0 to 63, all different within a row; in each aligned block of 48 rows (0 to 47, 48 to 95, ...) at most 10 rows name the same one
- gate_weights: float32 [1536, 6], P('dp'), may hold values from 0.02 to 0.5
Outputs:
- layer_out: bfloat16 [1536, 2048], P('dp', 'expert')
Inputs may be any that keep to these rules, and one draw needn't show every extreme that they name: `expert_ids`: each token names 6 different experts; among the 48 tokens of one index of dp (aligned blocks of rows) no expert is named by more than 10 tokens, a bound that some block reaches.
All inputs are finite; a program needn't handle non-finite values.
Results may differ from a plain program's by a relative error of at most 0.0035.
Values may be sent and summed in bfloat16 or wider, within the bound.
A program may use at most 128 MiB of HBM per device.

v0:
```python
import jax
import jax.numpy as jnp
from jax import lax
from jax.sharding import PartitionSpec as P

epsilon = 1e-06


def by_rows(left, right):
    return lax.dot_general(
        left, right, (((1,), (1,)), ((), ())), preferred_element_type=jnp.float32
    )


def expert_slots(expert_ids, experts, capacity):
    token_count, choose = expert_ids.shape
    flat_ids = expert_ids.reshape(-1)
    matches = (flat_ids[:, None] == jnp.arange(experts, dtype=jnp.int32)[None, :]).astype(jnp.int32)
    earlier = jnp.cumsum(matches, axis=0) - matches
    target = flat_ids * capacity + jnp.sum(earlier * matches, axis=1)
    return target.reshape(token_count, choose)


def collect_rows(returned_rows, slot_index, gate_weights):
    token_count, choose = slot_index.shape
    picked = returned_rows[slot_index.reshape(-1)].reshape(
        token_count, choose, returned_rows.shape[1]
    )
    return jnp.sum(picked * gate_weights[:, :, None], axis=1)


def expert_apply(buffer, expert_gate, expert_up, expert_down):
    gate_part = jnp.einsum(
        "slmd,lfd->slmf", buffer, expert_gate, preferred_element_type=jnp.float32
    )
    up_part = jnp.einsum("slmd,lfd->slmf", buffer, expert_up, preferred_element_type=jnp.float32)
    active = (jax.nn.silu(gate_part) * up_part).astype(jnp.bfloat16)
    return jnp.einsum("slmf,lfd->slmd", active, expert_down, preferred_element_type=jnp.float32)


def shards(
    residual_in,
    attention_values,
    out_weight,
    norm_gain,
    shared_gate,
    shared_up,
    shared_down,
    expert_gate,
    expert_up,
    expert_down,
    expert_ids,
    gate_weights,
):
    row_count = residual_in.shape[0]
    slice_width = residual_in.shape[1]
    expert_size = lax.axis_size("expert")
    batch_size = lax.axis_size("dp")
    full_width = slice_width * expert_size
    local_experts = expert_gate.shape[0]
    experts = local_experts * batch_size
    choose = expert_ids.shape[1]
    capacity = 2 * ((row_count * choose + experts - 1) // experts)
    column_start = lax.axis_index("expert") * slice_width
    head_terms = jnp.dot(
        attention_values,
        lax.all_gather(out_weight, "dp", axis=1, tiled=True),
        preferred_element_type=jnp.float32,
    )
    residual_own = residual_in.astype(jnp.float32)
    current = lax.dynamic_slice_in_dim(head_terms, column_start, slice_width, 1)
    head_terms = lax.dynamic_update_slice_in_dim(
        head_terms, current + residual_own, column_start, 1
    )
    residual = lax.psum(head_terms, "expert")
    inverse_rms = lax.rsqrt(jnp.mean(residual * residual, axis=1, keepdims=True) + epsilon)
    normed = (residual * inverse_rms * norm_gain).astype(jnp.bfloat16)
    residual_slice = lax.dynamic_slice_in_dim(residual, column_start, slice_width, 1)
    shared_active = (jax.nn.silu(by_rows(normed, shared_gate)) * by_rows(normed, shared_up)).astype(
        jnp.bfloat16
    )
    shared_terms = jnp.dot(shared_active, shared_down, preferred_element_type=jnp.float32)
    slot_index = expert_slots(expert_ids, experts, capacity)
    places = (
        slot_index[:, :, None] == jnp.arange(experts * capacity, dtype=jnp.int32)[None, None, :]
    )
    selector = jnp.any(places, axis=1).astype(jnp.bfloat16)
    slot_rows = lax.dot_general(
        selector, normed, (((0,), (0,)), ((), ())), preferred_element_type=jnp.float32
    )
    buffer = slot_rows.astype(jnp.bfloat16).reshape(batch_size, local_experts, capacity, full_width)
    partials = expert_apply(
        lax.all_to_all(buffer, "dp", split_axis=0, concat_axis=0, tiled=True),
        expert_gate,
        expert_up,
        expert_down,
    )
    returned = lax.all_to_all(partials, "dp", split_axis=0, concat_axis=0, tiled=True)
    routed_terms = collect_rows(
        returned.reshape(experts * capacity, full_width), slot_index, gate_weights
    )
    totals = lax.psum_scatter(
        shared_terms + routed_terms, "expert", scatter_dimension=1, tiled=True
    )
    return (residual_slice + totals).astype(jnp.bfloat16)


def solution(mesh):
    return jax.shard_map(
        shards,
        mesh=mesh,
        in_specs=(
            P("dp", "expert"),
            P("dp", "expert"),
            P("expert", "dp"),
            P(),
            P("expert", None),
            P("expert", None),
            P("expert", None),
            P("dp", "expert", None),
            P("dp", "expert", None),
            P("dp", "expert", None),
            P("dp", None),
            P("dp", None),
        ),
        out_specs=P("dp", "expert"),
        check_vma=False,
    )
```

profile of v0, /device:TPU:32, one launch (start us, length us, event | category | flops | bytes accessed | tf_op | source)
XLA Modules:
  0.0 723.8 jit_solution(14739102939381321039)
XLA Ops:
  6.5 0.0 copy-start
  6.5 0.0 all-reduce.3.cloned.1.call-start
  6.5 81.4 %all_gather.3 = bf16[128,2048]{0,1:T(8,128)(2,1)S(1)} all-gather(bf16[128,64]{0,1:T(8,128)(2,1)} %param.14), channel_id=1, replica_groups=mesh['dp'=32,'expert'=16] {'dp'}, dimensions={1}, use_global_device_ids=true | all-gather | bytes 540672 | tf_op jit(solution)/shard_map/all_gather | solution.py:67
  87.9 1.0 fusion.42
  88.9 0.7 add_dynamic-update-slice_fusion
  89.6 0.7 copy-done.1
  90.4 0.0 all-reduce.3.cloned.1.call-update
  90.4 0.8 copy.41
  91.2 0.1 eq.35
  91.4 0.9 reduce-window.6
  92.3 0.2 slice_reduce_fusion
  92.5 0.1 bitcast_bitcast_fusion
  92.7 0.1 reduce_sum.33
  92.8 0.6 broadcast_multiply_fusion
  93.4 0.1 copy.45
  93.5 0.8 fusion.19
  94.3 121.7 %all-reduce.3.cloned.1.call-done = f32[48,2048]{1,0:T(8,128)} async-done(((f32[48,2048]{1,0:T(8,128)}), f32[48,2048]{1,0:T(8,128)}) %all-reduce.3.cloned.1.call-update) | async-done | bytes 393232 | tf_op jit(solution)/shard_map/psum | solution.py:75
  216.0 1.1 multiply_reduce_fusion.1
  217.1 0.0 copy-done.6
  217.1 1.1 multiply_convert_fusion
  218.3 1.6 convolution_convert_fusion
  219.9 2.8 reshape.68
  222.7 4.9 copy.46
  227.6 0.0 copy-start.8
  227.6 138.5 %all_to_all.10 = bf16[32,2,10,2048]{3,1,2,0:T(2,128)(2,1)S(1)} all-to-all(bf16[32,2,10,2048]{3,1,2,0:T(2,128)(2,1)S(1)} %copy.46), channel_id=1, replica_groups=mesh['dp'=32,'expert'=16] {'dp'}, dimensions={0} | all-to-all | bytes 5242880 | tf_op jit(solution)/shard_map/all_to_all | solution.py:93
  366.1 0.0 copy-done.8
  366.1 2.3 fusion.4
  368.4 0.0 copy-done
  368.4 5.9 convolution_bitcast_fusion
  374.3 8.8 %copy.49 = f32[32,2,10,2048]{3,1,2,0:T(2,128)} copy(f32[32,2,10,2048]{3,0,2,1:T(8,128)} %convolution_bitcast_fusion) | data formatting | bytes 10485760 | tf_op jit(solution)/shard_map/slmf,lfd->slmd/transpose | solution.py:38
  383.1 4.8 all-to-all-start.1
  387.9 0.3 reduce-scatter.2.cloned.1.call-start
  388.2 0.0 copy-done.5
  388.2 0.1 mul.78
  388.3 0.0 copy-done.7
  388.4 0.1 copy.51
  388.5 0.0 copy-done.4
  388.5 0.3 fusion.43
  388.8 234.1 %all-to-all-done.1 = f32[32,2,10,2048]{3,1,2,0:T(2,128)} async-done(((f32[32,2,10,2048]{3,1,2,0:T(2,128)}), f32[32,2,10,2048]{3,1,2,0:T(2,128)}, u32[]{:S(2)}, u32[]{:S(2)}) %all-to-all-start.1) | async-done | bytes 5242912 | tf_op jit(solution)/shard_map/all_to_all | solution.py:98
  623.0 10.3 %copy.50 = f32[32,2,10,2048]{3,2,1,0:T(8,128)} copy(f32[32,2,10,2048]{3,1,2,0:T(2,128)} %all-to-all-done.1) | data formatting | bytes 10485760 | tf_op jit(solution)/shard_map/all_to_all | solution.py:98
  633.3 7.4 %reshape.69 = f32[640,2048]{1,0:T(8,128)} reshape(f32[32,2,10,2048]{3,2,1,0:T(8,128)} %copy.50) | data formatting | bytes 10485760 | tf_op jit(solution)/shard_map/reshape | solution.py:100
  640.7 6.8 gather_fusion
  647.4 1.8 reshape.70
  649.3 3.1 multiply_reduce_fusion
  652.5 1.4 convolution_add_fusion
  653.9 0.0 reduce-scatter.2.cloned.1.call-update
  653.9 61.7 %reduce-scatter.2.cloned.1.call-done = f32[48,128]{1,0:T(8,128)} async-done(((f32[48,2048]{1,0:T(8,128)}), f32[48,128]{1,0:T(8,128)}) %reduce-scatter.2.cloned.1.call-update) | async-done | bytes 24592 | tf_op jit(solution)/shard_map/reduce_scatter | solution.py:102
  715.6 1.4 add_convert_fusion
  (16 shorter events, 0.2 us)
Async XLA Ops:
  6.5 361.9 %copy-start = (bf16[2,88,2048]{2,1,0:T(8,128)(2,1)S(1)}, bf16[2,88,2048]{2,1,0:T(8,128)(2,1)}, u32[]{:S(2)}) copy-start(bf16[2,88,2048]{2,1,0:T(8,128)(2,1)} %param.21) | copy-start | bytes 2162692
  6.5 210.6 %copy-start.6 = (f32[2048]{0:T(1024)S(1)}, f32[2048]{0:T(1024)}, u32[]{:S(2)}) copy-start(f32[2048]{0:T(1024)} %param.15) | copy-start | bytes 24580
  6.5 209.5 %all-reduce.3.cloned.1.call-start = ((), (), s32[]{:S(2)}) async-start(), calls=%async_computation.3 | async-start | bytes 786432 | tf_op jit(solution)/shard_map/psum | solution.py:75
  89.6 0.7 copy-start.1
  227.6 138.5 %copy-start.8 = (bf16[2,88,2048]{2,1,0:T(8,128)(2,1)S(1)}, bf16[2,88,2048]{2,1,0:T(8,128)(2,1)}, u32[]{:S(2)}) copy-start(bf16[2,88,2048]{2,1,0:T(8,128)(2,1)} %param.19) | copy-start | bytes 2162692
  383.1 5.1 copy-start.5
  383.1 5.2 copy-start.7
  383.1 5.4 copy-start.4
  383.1 239.9 %all-to-all-start.1 = ((f32[32,2,10,2048]{3,1,2,0:T(2,128)}), f32[32,2,10,2048]{3,1,2,0:T(2,128)}, u32[]{:S(2)}, u32[]{:S(2)}) async-start(f32[32,2,10,2048]{3,1,2,0:T(2,128)} %copy.49), calls=%async_computation.1 | async-start | bytes 10485760 | tf_op jit(solution)/shard_map/all_to_all | solution.py:98
  387.9 327.7 %reduce-scatter.2.cloned.1.call-start = ((), (), s32[]{:S(2)}) async-start(), calls=%async_computation.4 | async-start | bytes 417792 | tf_op jit(solution)/shard_map/reduce_scatter | solution.py:102
  649.3 3.1 copy-start.2
  649.3 3.2 copy-start.3
Sparse Core Ops, SparseCore 0:
  90.5 125.4 all-reduce.2
  654.0 61.5 reduce-scatter.1
where the time goes:
time: 725 us; the launch traced here: 724 us
  waiting for transfers between devices  418 us (58%)
  blocking collectives  220 us (30%)
  local copies, waits for them, and re-layouts  45.1 us (6%)
  between operations  13.6 us (2%)
  matrix products  12.6 us (2%)
  other arithmetic  9.98 us (1%)
    all_to_all x1, waiting for transfers between devices, shards(): lax.all_to_all(partials, 'dp', split_axis=0, concat_axis=0, tiled=True)  234 us
    all_to_all x1, blocking collectives, shards(): lax.all_to_all(buffer, 'dp', split_axis=0, concat_axis=0, tiled=True)  138 us
    psum x1, waiting for transfers between devices, shards(): residual = lax.psum(head_terms, 'expert')  122 us
    all_gather x1, blocking collectives, shards(): lax.all_gather(out_weight, 'dp', axis=1, tiled=True)  81.4 us
    reduce_scatter x1, waiting for transfers between devices, shards(): lax.psum_scatter(shared_terms + routed_terms, 'expert', scatter_dimension...  61.7 us
  transfers between devices with their start and end apart: 3, of which 3 were waited for; matrix products, arithmetic and copies ran while one was open for 1% of the time, Pallas kernels for 0%

commit v1 on v0

--- a/solution.py
+++ b/solution.py
@@ -62,10 +62,17 @@
     choose = expert_ids.shape[1]
     capacity = 2 * ((row_count * choose + experts - 1) // experts)
     column_start = lax.axis_index("expert") * slice_width
+    update_slabs = lambda body, a_name, dim_at: jnp.concatenate(
+        jax.lax.all_to_all(
+            jnp.stack(jax.lax.axis_size(a_name) * [body], axis=0),
+            a_name,
+            split_axis=0,
+            concat_axis=0,
+        ),
+        axis=dim_at,
+    )
     head_terms = jnp.dot(
-        attention_values,
-        lax.all_gather(out_weight, "dp", axis=1, tiled=True),
-        preferred_element_type=jnp.float32,
+        attention_values, update_slabs(out_weight, "dp", 1), preferred_element_type=jnp.float32
     )
     residual_own = residual_in.astype(jnp.float32)
     current = lax.dynamic_slice_in_dim(head_terms, column_start, slice_width, 1)

time: 725 us -> 693 us (0.956)
  blocking collectives: 220 us -> 138 us
  waiting for transfers between devices: 418 us -> 449 us
  starting transfers between devices: 5.08 us -> 23.1 us
    all_gather x1 -> x0, blocking collectives: 81.4 us -> none  [shards(): lax.all_gather(out_weight, 'dp', axis=1, tiled=True)]
    all_to_all x0 -> x1, waiting for transfers between devices: none -> 31.5 us  [shards(): jax.lax.all_to_all(jnp.stack(jax.lax.axis_size(a_name) * [body], axis=0),...]
    all_to_all x0 -> x1, starting transfers between devices: none -> 18 us  [shards(): jax.lax.all_to_all(jnp.stack(jax.lax.axis_size(a_name) * [body], axis=0),...]
  transfers between devices with their start and end apart: 3 -> 4, of which waited for: 3 -> 4; matrix products, arithmetic and copies ran while one was open for 1% -> 1% of each run, Pallas kernels for 0% -> 0%
where the time goes in v1:
time: 693 us
  waiting for transfers between devices  449 us (65%)
  blocking collectives  138 us (20%)
  local copies, waits for them, and re-layouts  46.8 us (7%)
  starting transfers between devices  23.1 us (3%)
  between operations  13.6 us (2%)
  matrix products  12.6 us (2%)
  other arithmetic  9.28 us (1%)
    all_to_all x1, waiting for transfers between devices, shards(): lax.all_to_all(partials, 'dp', split_axis=0, concat_axis=0, tiled=True)  234 us
    all_to_all x1, blocking collectives, shards(): lax.all_to_all(buffer, 'dp', split_axis=0, concat_axis=0, tiled=True)  138 us
    psum x1, waiting for transfers between devices, shards(): residual = lax.psum(head_terms, 'expert')  121 us
    reduce_scatter x1, waiting for transfers between devices, shards(): lax.psum_scatter(shared_terms + routed_terms, 'expert', scatter_dimension...  61.7 us
    all_to_all x1, waiting for transfers between devices, shards(): jax.lax.all_to_all(jnp.stack(jax.lax.axis_size(a_name) * [body], axis=0),...  31.5 us
    all_to_all x1, starting transfers between devices, shards(): jax.lax.all_to_all(jnp.stack(jax.lax.axis_size(a_name) * [body], axis=0),...  18 us
  transfers between devices with their start and end apart: 4, of which 4 were waited for; matrix products, arithmetic and copies ran while one was open for 1% of the time, Pallas kernels for 0%

profile of v1, /device:TPU:32, one launch (start us, length us, event | category | flops | bytes accessed | tf_op | source)
XLA Modules:
  0.0 692.6 jit_solution(11471674108439746547)
XLA Ops:
  6.5 0.0 copy-start
  6.5 1.7 stack.2
  8.2 18.0 %all-to-all-start = ((bf16[32,128,64]{1,2,0:T(8,128)(2,1)}), bf16[32,128,64]{1,2,0:T(8,128)(2,1)S(1)}, u32[]{:S(2)}, u32[]{:S(2)}) async-start(bf16[32,128,64]{1,2,0:T(8,128)(2,1)} %stack.2), calls=%async_computation | async-start | bytes 1048576 | tf_op jit(solution)/shard_map/all_to_all | solution.py:66
  26.2 0.0 all-reduce.3.cloned.1.call-start
  26.3 0.8 copy.42
  27.1 0.1 eq.35
  27.2 0.9 reduce-window.6
  28.1 0.2 slice_reduce_fusion
  28.4 0.1 bitcast_bitcast_fusion
  28.5 31.5 %all-to-all-done = bf16[32,128,64]{1,2,0:T(8,128)(2,1)S(1)} async-done(((bf16[32,128,64]{1,2,0:T(8,128)(2,1)}), bf16[32,128,64]{1,2,0:T(8,128)(2,1)S(1)}, u32[]{:S(2)}, u32[]{:S(2)}) %all-to-all-start) | async-done | bytes 524320 | tf_op jit(solution)/shard_map/all_to_all | solution.py:66
  60.0 1.0 fusion.42
  61.0 0.0 copy-done.6
  61.0 0.0 copy-start.1
  61.0 0.7 copy-done.1
  61.7 0.0 all-reduce.3.cloned.1.call-update
  61.8 0.1 reduce_sum.33
  61.9 0.6 broadcast_multiply_fusion
  62.5 0.1 copy.46
  62.6 0.8 fusion.19
  63.4 121.4 %all-reduce.3.cloned.1.call-done = f32[48,2048]{1,0:T(8,128)} async-done(((f32[48,2048]{1,0:T(8,128)}), f32[48,2048]{1,0:T(8,128)}) %all-reduce.3.cloned.1.call-update) | async-done | bytes 393232 | tf_op jit(solution)/shard_map/psum | solution.py:82
  184.7 1.1 multiply_reduce_fusion.1
  185.9 0.0 copy-done.7
  185.9 1.1 multiply_convert_fusion
  187.0 1.6 convolution_convert_fusion
  188.6 2.8 reshape.78
  191.4 4.9 copy.47
  196.3 0.0 copy-start.9
  196.4 138.5 %all_to_all.15 = bf16[32,2,10,2048]{3,1,2,0:T(2,128)(2,1)S(1)} all-to-all(bf16[32,2,10,2048]{3,1,2,0:T(2,128)(2,1)S(1)} %copy.47), channel_id=1, replica_groups=mesh['dp'=32,'expert'=16] {'dp'}, dimensions={0} | all-to-all | bytes 5242880 | tf_op jit(solution)/shard_map/all_to_all | solution.py:100
  334.8 0.0 copy-done.9
  334.8 2.3 fusion.4
  337.1 5.9 convolution_bitcast_fusion
  343.0 8.8 %copy.50 = f32[32,2,10,2048]{3,1,2,0:T(2,128)} copy(f32[32,2,10,2048]{3,0,2,1:T(8,128)} %convolution_bitcast_fusion) | data formatting | bytes 10485760 | tf_op jit(solution)/shard_map/slmf,lfd->slmd/transpose | solution.py:38
  351.9 4.8 all-to-all-start.2
  356.7 0.3 reduce-scatter.2.cloned.1.call-start
  357.0 0.1 mul.78
  357.1 0.0 copy-done.8
  357.1 0.1 copy.52
  357.3 0.3 fusion.43
  357.6 234.1 %all-to-all-done.2 = f32[32,2,10,2048]{3,1,2,0:T(2,128)} async-done(((f32[32,2,10,2048]{3,1,2,0:T(2,128)}), f32[32,2,10,2048]{3,1,2,0:T(2,128)}, u32[]{:S(2)}, u32[]{:S(2)}) %all-to-all-start.2) | async-done | bytes 5242912 | tf_op jit(solution)/shard_map/all_to_all | solution.py:105
  591.7 10.3 %copy.51 = f32[32,2,10,2048]{3,2,1,0:T(8,128)} copy(f32[32,2,10,2048]{3,1,2,0:T(2,128)} %all-to-all-done.2) | data formatting | bytes 10485760 | tf_op jit(solution)/shard_map/all_to_all | solution.py:105
  602.0 7.4 %reshape.79 = f32[640,2048]{1,0:T(8,128)} reshape(f32[32,2,10,2048]{3,2,1,0:T(8,128)} %copy.51) | data formatting | bytes 10485760 | tf_op jit(solution)/shard_map/reshape | solution.py:107
  609.4 6.8 gather_fusion
  616.2 1.8 reshape.80
  618.0 3.1 multiply_reduce_fusion
  621.2 1.4 convolution_add_fusion
  622.6 0.0 reduce-scatter.2.cloned.1.call-update
  622.7 61.7 %reduce-scatter.2.cloned.1.call-done = f32[48,128]{1,0:T(8,128)} async-done(((f32[48,2048]{1,0:T(8,128)}), f32[48,128]{1,0:T(8,128)}) %reduce-scatter.2.cloned.1.call-update) | async-done | bytes 24592 | tf_op jit(solution)/shard_map/reduce_scatter | solution.py:109
  684.4 1.4 add_convert_fusion
  (20 shorter events, 0.2 us)
Async XLA Ops:
  6.5 330.6 %copy-start = (bf16[2,88,2048]{2,1,0:T(8,128)(2,1)S(1)}, bf16[2,88,2048]{2,1,0:T(8,128)(2,1)}, u32[]{:S(2)}) copy-start(bf16[2,88,2048]{2,1,0:T(8,128)(2,1)} %param.21) | copy-start | bytes 2162692
  6.5 54.4 %copy-start.6 = (bf16[48,128]{1,0:T(8,128)(2,1)S(1)}, bf16[48,128]{1,0:T(8,128)(2,1)}, u32[]{:S(2)}) copy-start(bf16[48,128]{1,0:T(8,128)(2,1)} %param.12) | copy-start | bytes 36868
  6.5 179.3 %copy-start.7 = (f32[2048]{0:T(1024)S(1)}, f32[2048]{0:T(1024)}, u32[]{:S(2)}) copy-start(f32[2048]{0:T(1024)} %param.15) | copy-start | bytes 24580
  8.2 51.7 %all-to-all-start = ((bf16[32,128,64]{1,2,0:T(8,128)(2,1)}), bf16[32,128,64]{1,2,0:T(8,128)(2,1)S(1)}, u32[]{:S(2)}, u32[]{:S(2)}) async-start(bf16[32,128,64]{1,2,0:T(8,128)(2,1)} %stack.2), calls=%async_computation | async-start | bytes 1048576 | tf_op jit(solution)/shard_map/all_to_all | solution.py:66
  26.2 158.5 %all-reduce.3.cloned.1.call-start = ((), (), s32[]{:S(2)}) async-start(), calls=%async_computation.4 | async-start | bytes 786432 | tf_op jit(solution)/shard_map/psum | solution.py:82
  61.0 0.7 copy-start.1
  196.3 138.5 %copy-start.9 = (bf16[2,88,2048]{2,1,0:T(8,128)(2,1)S(1)}, bf16[2,88,2048]{2,1,0:T(8,128)(2,1)}, u32[]{:S(2)}) copy-start(bf16[2,88,2048]{2,1,0:T(8,128)(2,1)} %param.19) | copy-start | bytes 2162692
  351.9 5.1 copy-start.5
  351.9 5.3 copy-start.8
  351.9 5.4 copy-start.4
  351.9 239.9 %all-to-all-start.2 = ((f32[32,2,10,2048]{3,1,2,0:T(2,128)}), f32[32,2,10,2048]{3,1,2,0:T(2,128)}, u32[]{:S(2)}, u32[]{:S(2)}) async-start(f32[32,2,10,2048]{3,1,2,0:T(2,128)} %copy.50), calls=%async_computation.2 | async-start | bytes 10485760 | tf_op jit(solution)/shard_map/all_to_all | solution.py:105
  356.7 327.7 %reduce-scatter.2.cloned.1.call-start = ((), (), s32[]{:S(2)}) async-start(), calls=%async_computation.5 | async-start | bytes 417792 | tf_op jit(solution)/shard_map/reduce_scatter | solution.py:109
  618.0 3.1 copy-start.2
  618.0 3.2 copy-start.3
Sparse Core Ops, SparseCore 0:
  61.9 122.8 all-reduce.2
  622.8 61.5 reduce-scatter.1
